TPU v7x, 32 devices: a whole 2x2x4 slice. The times are simulated.
32 devices in a mesh: real: 2 (over x), tile: 16 (over z, y, core).
Axes of the slice: x: 2, y: 2, z: 4, core: 2. Of those that a mesh axis runs over, the one named last changes fastest.
Arguments:
- positions: float32 [6, 8192], P('real', 'tile'), parts along dimension 0, may hold values from -1.5 to 125.5, as said below
- residual: float32 [6, 8192], P('real', 'tile'), parts along dimension 0, may hold values from -24 to 24
- iterate: float32 [6, 8192], P('real', 'tile'), parts along dimension 0, may hold values from -6 to 6
Outputs:
- new_iterate: float32 [6, 8192], P('real', 'tile'), parts along dimension 0
- new_residual: float32 [6, 8192], P('real', 'tile'), parts along dimension 0
- new_direction: float32 [6, 8192], P('real', 'tile'), parts along dimension 0
There are 2 independent parts, one for each index of `real`. A program takes and returns all parts, laid end to end along the dimension named above; each array names one. Nothing has to cross between parts.
Inputs may be any that keep to these rules, and one draw needn't show every extreme that they name: `positions`: distinct blobs are at least 1 apart.
All inputs are finite; a program needn't handle non-finite values.
Results may differ from a plain program's by a relative error of at most 0.0003.
Values sent between devices are 32-bit elements; how exact they have to be, the bound alone decides.
A program may use at most 64 MiB of HBM per device.

v0:
```python
import jax
import jax.numpy as jnp
from jax import lax
from jax.sharding import PartitionSpec as P


def pair_terms(row_pos, col_pos):
    separation = row_pos[:, :, None] - col_pos[:, None, :]
    squared = jnp.sum(separation * separation, axis=0)
    radius = jnp.sqrt(squared)
    inverse = 1.0 / jnp.maximum(radius, 0.5)
    inverse_sq = inverse * inverse
    far_scalar = 0.75 * inverse * (1.0 + 2.0 / 3.0 * inverse_sq)
    far_tensor = 0.75 * (1.0 - 2.0 * inverse_sq) * inverse_sq * inverse
    touching = radius < 2.0
    scalar_part = jnp.where(touching, 1.0 - 9.0 / 32.0 * radius, far_scalar)
    tensor_part = jnp.where(touching, 3.0 / 32.0 * inverse, far_tensor)
    return (separation, scalar_part, tensor_part)


def toward_rows(separation, scalar_part, tensor_part, col_forces):
    projected = jnp.sum(separation * col_forces[:, None, :], axis=0)
    return jnp.sum(
        scalar_part[None] * col_forces[:, None, :] + (tensor_part * projected)[None] * separation,
        axis=2,
    )


def shards(positions, residual, iterate):
    own_blobs = positions.shape[1]
    old_norm = lax.psum(jnp.sum(residual * residual), "tile")
    col_pos = lax.all_gather(positions, "tile", axis=1, tiled=True)
    col_forces = lax.all_gather(residual, "tile", axis=1, tiled=True)
    portion_cols = col_pos.shape[1]
    col_block = portion_cols
    for factor in (4, 2, 1):
        col_block = factor * own_blobs
        break

    def add_block(turn_index, running):
        block_pos = lax.dynamic_slice_in_dim(col_pos, turn_index * col_block, col_block, 1)
        block_forces = lax.dynamic_slice_in_dim(col_forces, turn_index * col_block, col_block, 1)
        separation, scalar_part, tensor_part = pair_terms(positions, block_pos)
        return running + toward_rows(separation, scalar_part, tensor_part, block_forces)

    applied = lax.fori_loop(0, portion_cols // col_block, add_block, jnp.zeros_like(residual))
    curvature = lax.psum(jnp.sum(residual * applied), "tile")
    step_size = old_norm / curvature
    new_residual = residual - step_size * applied
    new_norm = lax.psum(jnp.sum(new_residual * new_residual), "tile")
    new_iterate = iterate + step_size * residual
    new_direction = new_residual + new_norm / old_norm * residual
    return (new_iterate, new_residual, new_direction)


def solution(mesh):
    return jax.shard_map(
        shards,
        mesh=mesh,
        in_specs=(P("real", "tile"), P("real", "tile"), P("real", "tile")),
        out_specs=(P("real", "tile"), P("real", "tile"), P("real", "tile")),
        check_vma=False,
    )
```

profile of v0, /device:TPU:0, one launch (start us, length us, event | category | flops | bytes accessed | tf_op | source)
XLA Modules:
  0.0 165.1 jit_solution(6442482215898881509)
XLA Ops:
  0.6 23.7 %all_gather.6 = f32[3,8192]{1,0:T(4,128)S(1)} all-gather(f32[3,512]{1,0:T(4,128)} %param.5), channel_id=1, replica_groups=mesh['real'=2,'tile'=16] {'tile'}, dimensions={1}, use_global_device_ids=true | all-gather | bytes 104448 | tf_op jit(solution)/shard_map/all_gather | solution.py:32
  24.3 18.0 %all_gather.7 = f32[3,8192]{1,0:T(4,128)S(1)} all-gather(f32[3,512]{1,0:T(4,128)} %param.6), channel_id=1, replica_groups=mesh['real'=2,'tile'=16] {'tile'}, dimensions={1}, use_global_device_ids=true | all-gather | bytes 104448 | tf_op jit(solution)/shard_map/all_gather | solution.py:33
  42.4 0.0 copy-start.1
  42.4 56.4 %while.14 = (s32[]{:T(128)}, f32[3,512]{1,0:T(4,128)S(1)}, f32[3,512]{1,0:T(4,128)}, f32[3,8192]{1,0:T(4,128)S(1)}, f32[3,8192]{1,0:T(4,128)S(1)}, /*index=5*/s32[]{:T(128)}, s32[]{:T(128)}, s32[]{:T(128)}, s32[]{:T(128)}) while((s32[]{:T(128)}, f32[3,512]{1,0:T(4,128)S(1)}, f32[3,512]{1,0:T(4,128)}, f32[3,8192]{1,0:T(4,128)S(1)}, ...), condition=%wide.region_6.7_spmd.clone, body=%wide.region_2.6_spmd.clone.sunk | while | flops 49284612 | bytes 33812656 | solution.py:46
  42.4 8.2 %fusion.10 = (f32[512,2048]{1,0:T(8,128)S(1)}, f32[512,2048]{1,0:T(8,128)S(1)}) fusion(f32[3,2048]{1,0:T(4,128)S(1)} %get-tuple-element.177, f32[3,512]{1,0:T(4,128)} %get-tuple-element.203, f32[3,2048]{1,0:T(4,128)S(1)} %get-tuple-element.178), kind=kLoop, calls=%fused_computation.3.clone.1 | loop fusion | flops 13631488 | bytes 8443904 | tf_op jit(solution)/shard_map/while/body/eval_jaxpr/reduce_sum | solution.py:9
  50.6 0.0 copy-start
  50.6 3.6 %fusion.11 = (f32[512,2048]{1,0:T(8,128)S(1)}, f32[512,2048]{1,0:T(8,128)S(1)}) fusion(f32[512,2048]{1,0:T(8,128)S(1)} %get-tuple-element.179, f32[512,2048]{1,0:T(8,128)S(1)} %get-tuple-element.180), kind=kLoop, calls=%fused_computation.11.clone.1 | loop fusion | flops 19922944 | bytes 16777216 | tf_op jit(solution)/shard_map/while/body/eval_jaxpr/jit(_where)/select_n | solution.py:16
  54.2 0.0 copy-done
  54.2 2.3 %fusion.12 = f32[3,512]{1,0:T(4,128)S(1)} fusion(f32[512,2048]{1,0:T(8,128)S(1)} %get-tuple-element.181, f32[3,2048]{1,0:T(4,128)S(1)} %get-tuple-element.178, f32[512,2048]{1,0:T(8,128)S(1)} %get-tuple-element.182, f32[3,2048]{1,0:T(4,128)S(1)} %get-tuple-element.177, f32[3,512]{1,0:T(4,128)S(1)} %copy-done), kind=kLoop, calls=%fused_computation.6.clone.1 | loop fusion | flops 15727104 | bytes 8450048 | tf_op jit(solution)/shard_map/while/body/eval_jaxpr/reduce_sum | solution.py:23
  56.5 8.2 %fusion.10 = (f32[512,2048]{1,0:T(8,128)S(1)}, f32[512,2048]{1,0:T(8,128)S(1)}) fusion(f32[3,2048]{1,0:T(4,128)S(1)} %get-tuple-element.177, f32[3,512]{1,0:T(4,128)} %get-tuple-element.203, f32[3,2048]{1,0:T(4,128)S(1)} %get-tuple-element.178), kind=kLoop, calls=%fused_computation.3.clone.1 | loop fusion | flops 13631488 | bytes 8443904 | tf_op jit(solution)/shard_map/while/body/eval_jaxpr/reduce_sum | solution.py:9
  64.7 0.0 copy-start
  64.7 3.6 %fusion.11 = (f32[512,2048]{1,0:T(8,128)S(1)}, f32[512,2048]{1,0:T(8,128)S(1)}) fusion(f32[512,2048]{1,0:T(8,128)S(1)} %get-tuple-element.179, f32[512,2048]{1,0:T(8,128)S(1)} %get-tuple-element.180), kind=kLoop, calls=%fused_computation.11.clone.1 | loop fusion | flops 19922944 | bytes 16777216 | tf_op jit(solution)/shard_map/while/body/eval_jaxpr/jit(_where)/select_n | solution.py:16
  68.3 0.0 copy-done
  68.3 2.3 %fusion.12 = f32[3,512]{1,0:T(4,128)S(1)} fusion(f32[512,2048]{1,0:T(8,128)S(1)} %get-tuple-element.181, f32[3,2048]{1,0:T(4,128)S(1)} %get-tuple-element.178, f32[512,2048]{1,0:T(8,128)S(1)} %get-tuple-element.182, f32[3,2048]{1,0:T(4,128)S(1)} %get-tuple-element.177, f32[3,512]{1,0:T(4,128)S(1)} %copy-done), kind=kLoop, calls=%fused_computation.6.clone.1 | loop fusion | flops 15727104 | bytes 8450048 | tf_op jit(solution)/shard_map/while/body/eval_jaxpr/reduce_sum | solution.py:23
  70.6 8.2 %fusion.10 = (f32[512,2048]{1,0:T(8,128)S(1)}, f32[512,2048]{1,0:T(8,128)S(1)}) fusion(f32[3,2048]{1,0:T(4,128)S(1)} %get-tuple-element.177, f32[3,512]{1,0:T(4,128)} %get-tuple-element.203, f32[3,2048]{1,0:T(4,128)S(1)} %get-tuple-element.178), kind=kLoop, calls=%fused_computation.3.clone.1 | loop fusion | flops 13631488 | bytes 8443904 | tf_op jit(solution)/shard_map/while/body/eval_jaxpr/reduce_sum | solution.py:9
  78.8 0.0 copy-start
  78.8 3.6 %fusion.11 = (f32[512,2048]{1,0:T(8,128)S(1)}, f32[512,2048]{1,0:T(8,128)S(1)}) fusion(f32[512,2048]{1,0:T(8,128)S(1)} %get-tuple-element.179, f32[512,2048]{1,0:T(8,128)S(1)} %get-tuple-element.180), kind=kLoop, calls=%fused_computation.11.clone.1 | loop fusion | flops 19922944 | bytes 16777216 | tf_op jit(solution)/shard_map/while/body/eval_jaxpr/jit(_where)/select_n | solution.py:16
  82.4 0.0 copy-done
  82.4 2.3 %fusion.12 = f32[3,512]{1,0:T(4,128)S(1)} fusion(f32[512,2048]{1,0:T(8,128)S(1)} %get-tuple-element.181, f32[3,2048]{1,0:T(4,128)S(1)} %get-tuple-element.178, f32[512,2048]{1,0:T(8,128)S(1)} %get-tuple-element.182, f32[3,2048]{1,0:T(4,128)S(1)} %get-tuple-element.177, f32[3,512]{1,0:T(4,128)S(1)} %copy-done), kind=kLoop, calls=%fused_computation.6.clone.1 | loop fusion | flops 15727104 | bytes 8450048 | tf_op jit(solution)/shard_map/while/body/eval_jaxpr/reduce_sum | solution.py:23
  84.7 8.2 %fusion.10 = (f32[512,2048]{1,0:T(8,128)S(1)}, f32[512,2048]{1,0:T(8,128)S(1)}) fusion(f32[3,2048]{1,0:T(4,128)S(1)} %get-tuple-element.177, f32[3,512]{1,0:T(4,128)} %get-tuple-element.203, f32[3,2048]{1,0:T(4,128)S(1)} %get-tuple-element.178), kind=kLoop, calls=%fused_computation.3.clone.1 | loop fusion | flops 13631488 | bytes 8443904 | tf_op jit(solution)/shard_map/while/body/eval_jaxpr/reduce_sum | solution.py:9
  92.9 0.0 copy-start
  92.9 3.6 %fusion.11 = (f32[512,2048]{1,0:T(8,128)S(1)}, f32[512,2048]{1,0:T(8,128)S(1)}) fusion(f32[512,2048]{1,0:T(8,128)S(1)} %get-tuple-element.179, f32[512,2048]{1,0:T(8,128)S(1)} %get-tuple-element.180), kind=kLoop, calls=%fused_computation.11.clone.1 | loop fusion | flops 19922944 | bytes 16777216 | tf_op jit(solution)/shard_map/while/body/eval_jaxpr/jit(_where)/select_n | solution.py:16
  96.5 0.0 copy-done
  96.5 2.3 %fusion.12 = f32[3,512]{1,0:T(4,128)S(1)} fusion(f32[512,2048]{1,0:T(8,128)S(1)} %get-tuple-element.181, f32[3,2048]{1,0:T(4,128)S(1)} %get-tuple-element.178, f32[512,2048]{1,0:T(8,128)S(1)} %get-tuple-element.182, f32[3,2048]{1,0:T(4,128)S(1)} %get-tuple-element.177, f32[3,512]{1,0:T(4,128)S(1)} %copy-done), kind=kLoop, calls=%fused_computation.6.clone.1 | loop fusion | flops 15727104 | bytes 8450048 | tf_op jit(solution)/shard_map/while/body/eval_jaxpr/reduce_sum | solution.py:23
  98.8 0.0 copy-done.1
  98.8 0.6 multiply_reduce_fusion.1
  99.4 31.7 %all-reduce = (f32[]{:T(128)}, f32[]{:T(128)}) all-reduce(f32[]{:T(128)} %get-tuple-element.119, f32[]{:T(128)} %get-tuple-element.118), channel_id=1, replica_groups=mesh['real'=2,'tile'=16] {'tile'}, use_global_device_ids=true, to_apply=%region_1.0 | all-reduce | flops 2 | bytes 16 | tf_op jit(solution)/shard_map/psum | solution.py:31
  132.5 0.6 multiply_reduce_fusion
  133.1 30.1 %psum.23 = f32[]{:T(128)} all-reduce(f32[]{:T(128)} %get-tuple-element.132), channel_id=1, replica_groups=mesh['real'=2,'tile'=16] {'tile'}, use_global_device_ids=true, to_apply=%region_10.11 | all-reduce | flops 1 | bytes 8 | tf_op jit(solution)/shard_map/psum | solution.py:50
  164.5 0.0 copy-done.3
  164.5 0.6 multiply_add_fusion
  165.1 0.0 copy-done.2
  (11 shorter events, 0.1 us)
Async XLA Ops:
  42.4 56.5 %copy-start.1 = (f32[3,512]{1,0:T(4,128)S(1)}, f32[3,512]{1,0:T(4,128)}, u32[]{:S(2)}) copy-start(f32[3,512]{1,0:T(4,128)} %param.6) | copy-start | bytes 18436
  42.4 122.2 %copy-start.3 = (f32[3,512]{1,0:T(4,128)S(1)}, f32[3,512]{1,0:T(4,128)}, u32[]{:S(2)}) copy-start(f32[3,512]{1,0:T(4,128)} %param.7) | copy-start | bytes 18436
  50.6 3.6 %copy-start = (f32[3,512]{1,0:T(4,128)S(1)}, f32[3,512]{1,0:T(4,128)}, u32[]{:S(2)}) copy-start(f32[3,512]{1,0:T(4,128)} %get-tuple-element.203) | copy-start | bytes 18436 | tf_op jit(solution)/shard_map/while
  64.7 3.6 %copy-start = (f32[3,512]{1,0:T(4,128)S(1)}, f32[3,512]{1,0:T(4,128)}, u32[]{:S(2)}) copy-start(f32[3,512]{1,0:T(4,128)} %get-tuple-element.203) | copy-start | bytes 18436 | tf_op jit(solution)/shard_map/while
  78.8 3.6 %copy-start = (f32[3,512]{1,0:T(4,128)S(1)}, f32[3,512]{1,0:T(4,128)}, u32[]{:S(2)}) copy-start(f32[3,512]{1,0:T(4,128)} %get-tuple-element.203) | copy-start | bytes 18436 | tf_op jit(solution)/shard_map/while
  92.9 3.6 %copy-start = (f32[3,512]{1,0:T(4,128)S(1)}, f32[3,512]{1,0:T(4,128)}, u32[]{:S(2)}) copy-start(f32[3,512]{1,0:T(4,128)} %get-tuple-element.203) | copy-start | bytes 18436 | tf_op jit(solution)/shard_map/while
  133.1 32.1 %copy-start.2 = (f32[3,512]{1,0:T(4,128)}, f32[3,512]{1,0:T(4,128)S(1)}, u32[]{:S(2)}) copy-start(f32[3,512]{1,0:T(4,128)S(1)} %get-tuple-element.133) | copy-start | bytes 18436
where the time goes:
time: 166 us; the launch traced here: 165 us
  blocking collectives  104 us (63%)
  other arithmetic  57.9 us (35%)
  between operations  3.34 us (2%)
    reduce_sum x4, other arithmetic, pair_terms(): squared = jnp.sum(separation * separation, axis=0)  32.7 us
    psum x1, blocking collectives, shards(): old_norm = lax.psum(jnp.sum(residual * residual), 'tile')  31.7 us
    psum x1, blocking collectives, shards(): new_norm = lax.psum(jnp.sum(new_residual * new_residual), 'tile')  30.1 us
    all_gather x1, blocking collectives, shards(): col_pos = lax.all_gather(positions, 'tile', axis=1, tiled=True)  23.7 us
    all_gather x1, blocking collectives, shards(): col_forces = lax.all_gather(residual, 'tile', axis=1, tiled=True)  18 us
    select_n x4, other arithmetic, pair_terms(): scalar_part = jnp.where(touching, 1.0 - 9.0 / 32.0 * radius, far_scalar)  14.3 us
    reduce_sum x4, other arithmetic, toward_rows(): jnp.sum(scalar_part[None] * col_forces[:, None, :] + (tensor_part * proje...  9.06 us

commit v1 on v0

--- a/solution.py
+++ b/solution.py
@@ -29,8 +29,11 @@
 def shards(positions, residual, iterate):
     own_blobs = positions.shape[1]
     old_norm = lax.psum(jnp.sum(residual * residual), "tile")
-    col_pos = lax.all_gather(positions, "tile", axis=1, tiled=True)
-    col_forces = lax.all_gather(residual, "tile", axis=1, tiled=True)
+    col_pos, col_forces = jnp.split(
+        lax.all_gather(jnp.concatenate([positions, residual], axis=0), "tile", axis=1, tiled=True),
+        [positions.shape[0]],
+        axis=0,
+    )
     portion_cols = col_pos.shape[1]
     col_block = portion_cols
     for factor in (4, 2, 1):

time: 166 us -> 147 us (0.89)
  blocking collectives: 104 us -> 84.4 us
    all_gather x2 -> x1, blocking collectives: 41.7 us -> 23.8 us  [shards(): lax.all_gather(jnp.concatenate([positions, residual], axis=0), 'tile', ax...]
where the time goes in v1:
time: 147 us
  blocking collectives  84.4 us (57%)
  other arithmetic  58.7 us (40%)
  between operations  3.36 us (2%)
    reduce_sum x4, other arithmetic, pair_terms(): squared = jnp.sum(separation * separation, axis=0)  32.7 us
    psum x1, blocking collectives, shards(): old_norm = lax.psum(jnp.sum(residual * residual), 'tile')  30.4 us
    psum x1, blocking collectives, shards(): new_norm = lax.psum(jnp.sum(new_residual * new_residual), 'tile')  30.1 us
    all_gather x1, blocking collectives, shards(): lax.all_gather(jnp.concatenate([positions, residual], axis=0), 'tile', ax...  23.8 us
    select_n x4, other arithmetic, pair_terms(): scalar_part = jnp.where(touching, 1.0 - 9.0 / 32.0 * radius, far_scalar)  14.3 us
    reduce_sum x4, other arithmetic, toward_rows(): jnp.sum(scalar_part[None] * col_forces[:, None, :] + (tensor_part * proje...  9.06 us

profile of v1, /device:TPU:0, one launch (start us, length us, event | category | flops | bytes accessed | tf_op | source)
XLA Modules:
  0.0 146.8 jit_solution(1465219236220859819)
XLA Ops:
  0.6 0.7 pad_maximum_fusion
  1.4 23.8 %all_gather.3 = f32[6,8192]{1,0:T(8,128)S(1)} all-gather(f32[6,512]{1,0:T(8,128)S(1)} %pad_maximum_fusion), channel_id=1, replica_groups=mesh['real'=2,'tile'=16] {'tile'}, dimensions={1}, use_global_device_ids=true | all-gather | bytes 208896 | tf_op jit(solution)/shard_map/all_gather | solution.py:33
  25.2 0.1 fusion.7
  25.2 0.0 copy-start.1
  25.3 0.0 copy-start.3
  25.3 56.5 %while.14 = (s32[]{:T(128)}, f32[3,512]{1,0:T(4,128)S(1)}, f32[3,512]{1,0:T(4,128)}, f32[3,8192]{1,0:T(4,128)S(1)}, f32[3,8192]{1,0:T(4,128)S(1)}, /*index=5*/s32[]{:T(128)}, s32[]{:T(128)}, s32[]{:T(128)}, s32[]{:T(128)}) while((s32[]{:T(128)}, f32[3,512]{1,0:T(4,128)S(1)}, f32[3,512]{1,0:T(4,128)}, f32[3,8192]{1,0:T(4,128)S(1)}, ...), condition=%wide.region_6.7_spmd.clone, body=%wide.region_2.6_spmd.clone.sunk | while | flops 49284612 | bytes 33812656 | solution.py:49
  25.3 8.2 %fusion.11 = (f32[512,2048]{1,0:T(8,128)S(1)}, f32[512,2048]{1,0:T(8,128)S(1)}) fusion(f32[3,2048]{1,0:T(4,128)S(1)} %get-tuple-element.179, f32[3,512]{1,0:T(4,128)} %get-tuple-element.205, f32[3,2048]{1,0:T(4,128)S(1)} %get-tuple-element.180), kind=kLoop, calls=%fused_computation.3.clone.1 | loop fusion | flops 13631488 | bytes 8443904 | tf_op jit(solution)/shard_map/while/body/eval_jaxpr/reduce_sum | solution.py:9
  33.5 0.0 copy-start
  33.5 3.6 %fusion.12 = (f32[512,2048]{1,0:T(8,128)S(1)}, f32[512,2048]{1,0:T(8,128)S(1)}) fusion(f32[512,2048]{1,0:T(8,128)S(1)} %get-tuple-element.181, f32[512,2048]{1,0:T(8,128)S(1)} %get-tuple-element.182), kind=kLoop, calls=%fused_computation.11.clone.1 | loop fusion | flops 19922944 | bytes 16777216 | tf_op jit(solution)/shard_map/while/body/eval_jaxpr/jit(_where)/select_n | solution.py:16
  37.1 0.0 copy-done
  37.1 2.3 %fusion.13 = f32[3,512]{1,0:T(4,128)S(1)} fusion(f32[512,2048]{1,0:T(8,128)S(1)} %get-tuple-element.183, f32[3,2048]{1,0:T(4,128)S(1)} %get-tuple-element.180, f32[512,2048]{1,0:T(8,128)S(1)} %get-tuple-element.184, f32[3,2048]{1,0:T(4,128)S(1)} %get-tuple-element.179, f32[3,512]{1,0:T(4,128)S(1)} %copy-done), kind=kLoop, calls=%fused_computation.6.clone.1 | loop fusion | flops 15727104 | bytes 8450048 | tf_op jit(solution)/shard_map/while/body/eval_jaxpr/reduce_sum | solution.py:23
  39.4 8.2 %fusion.11 = (f32[512,2048]{1,0:T(8,128)S(1)}, f32[512,2048]{1,0:T(8,128)S(1)}) fusion(f32[3,2048]{1,0:T(4,128)S(1)} %get-tuple-element.179, f32[3,512]{1,0:T(4,128)} %get-tuple-element.205, f32[3,2048]{1,0:T(4,128)S(1)} %get-tuple-element.180), kind=kLoop, calls=%fused_computation.3.clone.1 | loop fusion | flops 13631488 | bytes 8443904 | tf_op jit(solution)/shard_map/while/body/eval_jaxpr/reduce_sum | solution.py:9
  47.6 0.0 copy-start
  47.6 3.6 %fusion.12 = (f32[512,2048]{1,0:T(8,128)S(1)}, f32[512,2048]{1,0:T(8,128)S(1)}) fusion(f32[512,2048]{1,0:T(8,128)S(1)} %get-tuple-element.181, f32[512,2048]{1,0:T(8,128)S(1)} %get-tuple-element.182), kind=kLoop, calls=%fused_computation.11.clone.1 | loop fusion | flops 19922944 | bytes 16777216 | tf_op jit(solution)/shard_map/while/body/eval_jaxpr/jit(_where)/select_n | solution.py:16
  51.2 0.0 copy-done
  51.2 2.3 %fusion.13 = f32[3,512]{1,0:T(4,128)S(1)} fusion(f32[512,2048]{1,0:T(8,128)S(1)} %get-tuple-element.183, f32[3,2048]{1,0:T(4,128)S(1)} %get-tuple-element.180, f32[512,2048]{1,0:T(8,128)S(1)} %get-tuple-element.184, f32[3,2048]{1,0:T(4,128)S(1)} %get-tuple-element.179, f32[3,512]{1,0:T(4,128)S(1)} %copy-done), kind=kLoop, calls=%fused_computation.6.clone.1 | loop fusion | flops 15727104 | bytes 8450048 | tf_op jit(solution)/shard_map/while/body/eval_jaxpr/reduce_sum | solution.py:23
  53.5 8.2 %fusion.11 = (f32[512,2048]{1,0:T(8,128)S(1)}, f32[512,2048]{1,0:T(8,128)S(1)}) fusion(f32[3,2048]{1,0:T(4,128)S(1)} %get-tuple-element.179, f32[3,512]{1,0:T(4,128)} %get-tuple-element.205, f32[3,2048]{1,0:T(4,128)S(1)} %get-tuple-element.180), kind=kLoop, calls=%fused_computation.3.clone.1 | loop fusion | flops 13631488 | bytes 8443904 | tf_op jit(solution)/shard_map/while/body/eval_jaxpr/reduce_sum | solution.py:9
  61.7 0.0 copy-start
  61.7 3.6 %fusion.12 = (f32[512,2048]{1,0:T(8,128)S(1)}, f32[512,2048]{1,0:T(8,128)S(1)}) fusion(f32[512,2048]{1,0:T(8,128)S(1)} %get-tuple-element.181, f32[512,2048]{1,0:T(8,128)S(1)} %get-tuple-element.182), kind=kLoop, calls=%fused_computation.11.clone.1 | loop fusion | flops 19922944 | bytes 16777216 | tf_op jit(solution)/shard_map/while/body/eval_jaxpr/jit(_where)/select_n | solution.py:16
  65.3 0.0 copy-done
  65.3 2.3 %fusion.13 = f32[3,512]{1,0:T(4,128)S(1)} fusion(f32[512,2048]{1,0:T(8,128)S(1)} %get-tuple-element.183, f32[3,2048]{1,0:T(4,128)S(1)} %get-tuple-element.180, f32[512,2048]{1,0:T(8,128)S(1)} %get-tuple-element.184, f32[3,2048]{1,0:T(4,128)S(1)} %get-tuple-element.179, f32[3,512]{1,0:T(4,128)S(1)} %copy-done), kind=kLoop, calls=%fused_computation.6.clone.1 | loop fusion | flops 15727104 | bytes 8450048 | tf_op jit(solution)/shard_map/while/body/eval_jaxpr/reduce_sum | solution.py:23
  67.7 8.2 %fusion.11 = (f32[512,2048]{1,0:T(8,128)S(1)}, f32[512,2048]{1,0:T(8,128)S(1)}) fusion(f32[3,2048]{1,0:T(4,128)S(1)} %get-tuple-element.179, f32[3,512]{1,0:T(4,128)} %get-tuple-element.205, f32[3,2048]{1,0:T(4,128)S(1)} %get-tuple-element.180), kind=kLoop, calls=%fused_computation.3.clone.1 | loop fusion | flops 13631488 | bytes 8443904 | tf_op jit(solution)/shard_map/while/body/eval_jaxpr/reduce_sum | solution.py:9
  75.8 0.0 copy-start
  75.9 3.6 %fusion.12 = (f32[512,2048]{1,0:T(8,128)S(1)}, f32[512,2048]{1,0:T(8,128)S(1)}) fusion(f32[512,2048]{1,0:T(8,128)S(1)} %get-tuple-element.181, f32[512,2048]{1,0:T(8,128)S(1)} %get-tuple-element.182), kind=kLoop, calls=%fused_computation.11.clone.1 | loop fusion | flops 19922944 | bytes 16777216 | tf_op jit(solution)/shard_map/while/body/eval_jaxpr/jit(_where)/select_n | solution.py:16
  79.4 0.0 copy-done
  79.5 2.3 %fusion.13 = f32[3,512]{1,0:T(4,128)S(1)} fusion(f32[512,2048]{1,0:T(8,128)S(1)} %get-tuple-element.183, f32[3,2048]{1,0:T(4,128)S(1)} %get-tuple-element.180, f32[512,2048]{1,0:T(8,128)S(1)} %get-tuple-element.184, f32[3,2048]{1,0:T(4,128)S(1)} %get-tuple-element.179, f32[3,512]{1,0:T(4,128)S(1)} %copy-done), kind=kLoop, calls=%fused_computation.6.clone.1 | loop fusion | flops 15727104 | bytes 8450048 | tf_op jit(solution)/shard_map/while/body/eval_jaxpr/reduce_sum | solution.py:23
  81.7 0.0 copy-done.1
  81.8 0.6 multiply_reduce_fusion.1
  82.4 30.4 %all-reduce = (f32[]{:T(128)}, f32[]{:T(128)}) all-reduce(f32[]{:T(128)} %get-tuple-element.119, f32[]{:T(128)} %get-tuple-element.118), channel_id=1, replica_groups=mesh['real'=2,'tile'=16] {'tile'}, use_global_device_ids=true, to_apply=%region_1.0 | all-reduce | flops 2 | bytes 16 | tf_op jit(solution)/shard_map/psum | solution.py:31
  114.1 0.6 multiply_reduce_fusion
  114.8 30.1 %psum.23 = f32[]{:T(128)} all-reduce(f32[]{:T(128)} %get-tuple-element.132), channel_id=1, replica_groups=mesh['real'=2,'tile'=16] {'tile'}, use_global_device_ids=true, to_apply=%region_10.11 | all-reduce | flops 1 | bytes 8 | tf_op jit(solution)/shard_map/psum | solution.py:53
  146.2 0.6 multiply_add_fusion
  (12 shorter events, 0.1 us)
Async XLA Ops:
  25.2 56.5 %copy-start.1 = (f32[3,512]{1,0:T(4,128)S(1)}, f32[3,512]{1,0:T(4,128)}, u32[]{:S(2)}) copy-start(f32[3,512]{1,0:T(4,128)} %param.6) | copy-start | bytes 18436
  25.3 120.9 %copy-start.3 = (f32[3,512]{1,0:T(4,128)S(1)}, f32[3,512]{1,0:T(4,128)}, u32[]{:S(2)}) copy-start(f32[3,512]{1,0:T(4,128)} %param.7) | copy-start | bytes 18436
  33.5 3.6 %copy-start = (f32[3,512]{1,0:T(4,128)S(1)}, f32[3,512]{1,0:T(4,128)}, u32[]{:S(2)}) copy-start(f32[3,512]{1,0:T(4,128)} %get-tuple-element.205) | copy-start | bytes 18436 | tf_op jit(solution)/shard_map/while
  47.6 3.6 %copy-start = (f32[3,512]{1,0:T(4,128)S(1)}, f32[3,512]{1,0:T(4,128)}, u32[]{:S(2)}) copy-start(f32[3,512]{1,0:T(4,128)} %get-tuple-element.205) | copy-start | bytes 18436 | tf_op jit(solution)/shard_map/while
  61.7 3.6 %copy-start = (f32[3,512]{1,0:T(4,128)S(1)}, f32[3,512]{1,0:T(4,128)}, u32[]{:S(2)}) copy-start(f32[3,512]{1,0:T(4,128)} %get-tuple-element.205) | copy-start | bytes 18436 | tf_op jit(solution)/shard_map/while
  75.8 3.6 %copy-start = (f32[3,512]{1,0:T(4,128)S(1)}, f32[3,512]{1,0:T(4,128)}, u32[]{:S(2)}) copy-start(f32[3,512]{1,0:T(4,128)} %get-tuple-element.205) | copy-start | bytes 18436 | tf_op jit(solution)/shard_map/while
  114.8 32.1 %copy-start.2 = (f32[3,512]{1,0:T(4,128)}, f32[3,512]{1,0:T(4,128)S(1)}, u32[]{:S(2)}) copy-start(f32[3,512]{1,0:T(4,128)S(1)} %get-tuple-element.133) | copy-start | bytes 18436
